TPU v7x, 512 devices: a whole 4x4x16 slice. The times are simulated.
512 devices in a mesh: replica: 4 (over z_hi, core), inner: 128 (over z_lo, x, y).
Axes of the slice: x: 4, y: 4, z: 16 (z_hi: 2, z_lo: 8; z = z_hi * 8 + z_lo), core: 2. Of those that a mesh axis runs over, the one named last changes fastest.
Arguments:
- square_weights: float32 [2, 1024, 1024], P(None, 'inner'), may hold values from -6 to 6
- square_copies: float32 [4, 2, 1024, 1024], P('replica', None, 'inner'), may hold values from -6 to 6
- square_moment: float32 [2, 1024, 1024], P(None, 'inner'), may hold values from -6 to 6
- broad_weights: float32 [2, 1024, 2048], P(None, 'inner'), may hold values from -6 to 6
- broad_copies: float32 [4, 2, 1024, 2048], P('replica', None, 'inner'), may hold values from -6 to 6
- broad_moment: float32 [2, 1024, 2048], P(None, 'inner'), may hold values from -6 to 6
- embed_weights: float32 [16384, 1024], P('inner'), may hold values from -6 to 6
- embed_copies: float32 [4, 16384, 1024], P('replica', 'inner'), may hold values from -90 to 90, as said below
- embed_moment: float32 [16384, 1024], P('inner'), may hold values from -6 to 6
- embed_error: float32 [4, 16384, 1024], P('replica', 'inner'), may hold values from -3 to 3
- warm_start: float32 [64, 1024], replicated, may hold values from -6 to 6
Outputs:
- square_updated: float32 [2, 1024, 1024], P(None, 'inner')
- square_velocity: float32 [2, 1024, 1024], P(None, 'inner')
- broad_updated: float32 [2, 1024, 2048], P(None, 'inner')
- broad_velocity: float32 [2, 1024, 2048], P(None, 'inner')
- embed_updated: float32 [16384, 1024], P('inner')
- embed_velocity: float32 [16384, 1024], P('inner')
- embed_carried: float32 [4, 16384, 1024], P('replica', 'inner')
Inputs may be any that keep to these rules, and one draw needn't show every extreme that they name: `embed_copies`: each replica's embedding after its inner steps.
All inputs are finite; a program needn't handle non-finite values.
Results may differ from a plain program's by a relative error of at most 0.0001.
Values sent between devices are 32-bit elements; how exact they have to be, the bound alone decides.
A program may use at most 64 MiB of HBM per device.

v0:
```python
import jax
import jax.numpy as jnp
from jax import lax
from jax.sharding import PartitionSpec as P

outer_rate = 0.7
momentum_decay = 0.9


def nesterov(weights, gradient, moment):
    velocity = momentum_decay * moment + gradient
    return (weights - outer_rate * (gradient + momentum_decay * velocity), velocity)


def local(
    square_weights,
    square_copies,
    square_moment,
    broad_weights,
    broad_copies,
    broad_moment,
    embed_weights,
    embed_copies,
    embed_moment,
    embed_error,
    warm_start,
):
    replicas = lax.axis_size("replica")
    highest = lax.Precision.HIGHEST
    contract_last = (((1,), (1,)), ((), ()))
    square_term = square_weights - square_copies[0]
    broad_term = broad_weights - broad_copies[0]
    corrected = embed_weights - embed_copies[0] + embed_error[0]
    square_sum, broad_sum = lax.psum((square_term, broad_term), "replica")
    left_local = lax.dot_general(warm_start, corrected, contract_last, precision=highest)
    left_factor = lax.psum(left_local, "replica") / replicas
    gram_local = lax.dot_general(left_factor, left_factor, contract_last, precision=highest)
    gram_matrix = lax.psum(gram_local, "inner")
    lower_factor = jnp.linalg.cholesky(gram_matrix)
    basis_rows = lax.linalg.triangular_solve(lower_factor, left_factor, left_side=True, lower=True)
    right_term = jnp.dot(basis_rows, corrected, precision=highest)
    right_total = lax.psum(right_term, ("replica", "inner"))
    right_factor = right_total / replicas
    embed_step = lax.dot_general(
        basis_rows, right_factor, (((0,), (0,)), ((), ())), precision=highest
    )
    embed_updated, embed_velocity = nesterov(embed_weights, embed_step, embed_moment)
    square_updated, square_velocity = nesterov(square_weights, square_sum / replicas, square_moment)
    broad_updated, broad_velocity = nesterov(broad_weights, broad_sum / replicas, broad_moment)
    embed_carried = (corrected - embed_step)[None]
    return (
        square_updated,
        square_velocity,
        broad_updated,
        broad_velocity,
        embed_updated,
        embed_velocity,
        embed_carried,
    )


def solution(mesh):
    in_specs = (
        P(None, "inner", None),
        P("replica", None, "inner", None),
        P(None, "inner", None),
        P(None, "inner", None),
        P("replica", None, "inner", None),
        P(None, "inner", None),
        P("inner", None),
        P("replica", "inner", None),
        P("inner", None),
        P("replica", "inner", None),
        P(),
    )
    out_specs = (
        P(None, "inner", None),
        P(None, "inner", None),
        P(None, "inner", None),
        P(None, "inner", None),
        P("inner", None),
        P("inner", None),
        P("replica", "inner", None),
    )
    return jax.shard_map(local, mesh=mesh, in_specs=in_specs, out_specs=out_specs, check_vma=False)
```

profile of v0, /device:TPU:1, one launch (start us, length us, event | category | flops | bytes accessed | tf_op | source)
XLA Modules:
  0.0 1638.2 jit_solution(11594696563197630290)
XLA Ops:
  7.2 0.0 copy-start
  7.2 0.0 all-reduce.4.cloned.1.call-start
  7.2 1.5 bitcast_add_fusion
  8.7 0.0 copy-done
  8.7 0.7 convolution_bitcast_fusion
  9.4 33.8 %psum.37 = f32[64,128]{1,0:T(8,128)S(1)} all-reduce(f32[64,128]{1,0:T(8,128)S(1)} %convolution_bitcast_fusion), channel_id=1, replica_groups=mesh['replica'=4,'inner'=128] {'replica'}, use_global_device_ids=true, to_apply=%region_2.0 | all-reduce | flops 8192 | bytes 65536 | tf_op jit(solution)/shard_map/psum | solution.py:36
  43.2 0.2 fusion.8
  43.4 926.7 %psum.38 = f32[64,64]{0,1:T(8,128)S(1)} all-reduce(f32[64,64]{0,1:T(8,128)S(1)} %fusion.8), channel_id=1, replica_groups=mesh['replica'=4,'inner'=128] {'inner'}, use_global_device_ids=true, to_apply=%region_3.0 | all-reduce | flops 4096 | bytes 32768 | tf_op jit(solution)/shard_map/psum | solution.py:38
  970.1 0.1 copy.19
  970.2 5.8 cholesky.16
  976.1 0.6 compare_reduce_fusion
  976.7 0.7 fusion.3
  977.4 4.9 custom-call.6
  982.3 0.3 fusion.4
  982.5 0.0 copy-start.2
  982.5 0.0 copy-start.5
  982.6 0.0 copy-start.4
  982.6 0.0 copy-start.7
  982.6 1.1 fusion.17
  983.7 0.0 all-reduce.4.cloned.1.call-update
  983.8 0.0 all-reduce.6.cloned.1.call-start
  983.8 0.0 copy-done.2
  983.8 0.7 bitcast_subtract_fusion.1
  984.5 0.6 bitcast_subtract_fusion.2
  985.1 0.0 all-reduce.6.cloned.1.call-update
  985.2 0.0 copy-start.6
  985.2 561.2 %all-reduce.4.cloned.1.call-done = f32[64,1024]{1,0:T(8,128)} async-done(((f32[64,1024]{1,0:T(8,128)}), f32[64,1024]{1,0:T(8,128)}) %all-reduce.4.cloned.1.call-update) | async-done | bytes 262160 | tf_op jit(solution)/shard_map/psum | solution.py:42
  1546.4 2.8 multiply_subtract_fusion
  1549.2 79.8 %all-reduce.6.cloned.1.call-done = (f32[2,8,1024]{2,1,0:T(8,128)}, f32[2,8,2048]{2,1,0:T(8,128)}) async-done(((f32[2,8,1024]{2,1,0:T(8,128)}, f32[2,8,2048]{2,1,0:T(8,128)}), (f32[2,8,1024]{2,1,0:T(8,128)}, f32[2,8,2048]{2,1,0:T(8,128)})) %all-reduce.6.cloned.1.call-update) | async-done | bytes 196624 | tf_op jit(solution)/shard_map/psum | solution.py:34
  1629.1 1.7 multiply_subtract_fusion.1
  1630.7 0.0 copy-done.8
  1630.7 0.7 multiply_subtract_fusion.2
  (13 shorter events, 0.1 us)
Async XLA Ops:
  7.2 1.6 copy-start
  7.2 1539.2 %all-reduce.4.cloned.1.call-start = ((), (), s32[]{:S(2)}) async-start(), calls=%async_computation | async-start | bytes 524288 | tf_op jit(solution)/shard_map/psum | solution.py:42
  982.5 1.3 copy-start.2
  982.5 1.3 copy-start.5
  982.6 1.9 copy-start.4
  982.6 1.9 copy-start.7
  983.7 562.7 %copy-start.1 = (f32[128,1024]{1,0:T(8,128)S(1)}, f32[128,1024]{1,0:T(8,128)}, u32[]{:S(2)}) copy-start(f32[128,1024]{1,0:T(8,128)} %param.17) | copy-start | bytes 1572868
  983.7 562.7 %copy-start.3 = (f32[128,1024]{1,0:T(8,128)S(1)}, f32[128,1024]{1,0:T(8,128)}, u32[]{:S(2)}) copy-start(f32[128,1024]{1,0:T(8,128)} %param.19) | copy-start | bytes 1572868
  983.8 645.3 %all-reduce.6.cloned.1.call-start = ((), (), s32[]{:S(2)}) async-start(), calls=%async_computation.1 | async-start | bytes 393216 | tf_op jit(solution)/shard_map/psum | solution.py:34
  985.2 643.9 %copy-start.6 = (f32[2,8,2048]{2,1,0:T(8,128)S(1)}, f32[2,8,2048]{2,1,0:T(8,128)}, u32[]{:S(2)}) copy-start(f32[2,8,2048]{2,1,0:T(8,128)} %param.16) | copy-start | bytes 393220
  1629.1 1.7 copy-start.8
  1629.1 1.7 copy-start.9
Sparse Core Ops, SparseCore 0:
  983.9 562.4 all-reduce.3
  1550.2 78.7 all-reduce.5
where the time goes:
time: 1640 us
  blocking collectives  961 us (59%)
  waiting for transfers between devices  641 us (39%)
  other arithmetic  17.2 us (1%)
    psum x1, blocking collectives, local(): gram_matrix = lax.psum(gram_local, 'inner')  927 us
    psum x1, waiting for transfers between devices, local(): right_total = lax.psum(right_term, ('replica', 'inner'))  561 us
    psum x1, waiting for transfers between devices, local(): square_sum, broad_sum = lax.psum((square_term, broad_term), 'replica')  79.8 us
    psum x1, blocking collectives, local(): left_factor = lax.psum(left_local, 'replica') / replicas  33.8 us
  transfers between devices with their start and end apart: 2, of which 2 were waited for; matrix products, arithmetic and copies ran while one was open for 0% of the time, Pallas kernels for 0%

commit v1 on v0

--- a/solution.py
+++ b/solution.py
@@ -1,3 +1,4 @@
+import functools
 import jax
 import jax.numpy as jnp
 from jax import lax
@@ -5,6 +6,15 @@
 
 outer_rate = 0.7
 momentum_decay = 0.9
+
+
+def close_marks(mine, mesh_name, along_axis):
+    for num in (mesh_name, along_axis):
+        mine = jax.lax.psum(mine, num)
+    return mine
+
+
+shape_entries_now = functools.partial(close_marks, mesh_name="replica", along_axis="inner")
 
 
 def nesterov(weights, gradient, moment):
@@ -39,7 +49,7 @@
     lower_factor = jnp.linalg.cholesky(gram_matrix)
     basis_rows = lax.linalg.triangular_solve(lower_factor, left_factor, left_side=True, lower=True)
     right_term = jnp.dot(basis_rows, corrected, precision=highest)
-    right_total = lax.psum(right_term, ("replica", "inner"))
+    right_total = shape_entries_now(right_term)
     right_factor = right_total / replicas
     embed_step = lax.dot_general(
         basis_rows, right_factor, (((0,), (0,)), ((), ())), precision=highest

time: 1640 us -> 3020 us (1.84)
  waiting for transfers between devices: 641 us -> 1990 us
    psum x1, waiting for transfers between devices: 561 us -> 1800 us  [close_marks(): mine = jax.lax.psum(mine, num)]
    psum x1, waiting for transfers between devices: 79.8 us -> 198 us  [local(): square_sum, broad_sum = lax.psum((square_term, broad_term), 'replica')]
where the time goes in v1:
time: 3020 us; the launch traced here: 2990 us
  waiting for transfers between devices  1990 us (66%)
  blocking collectives  961 us (32%)
    psum x1, waiting for transfers between devices, close_marks(): mine = jax.lax.psum(mine, num)  1800 us
    psum x1, blocking collectives, local(): gram_matrix = lax.psum(gram_local, 'inner')  927 us
    psum x1, waiting for transfers between devices, local(): square_sum, broad_sum = lax.psum((square_term, broad_term), 'replica')  198 us
  transfers between devices with their start and end apart: 2, of which 2 were waited for; matrix products, arithmetic and copies ran while one was open for 0% of the time, Pallas kernels for 0%

profile of v1, /device:TPU:1, one launch (start us, length us, event | category | flops | bytes accessed | tf_op | source)
XLA Modules:
  0.0 2991.4 jit_solution(8751161365985808712)
XLA Ops:
  7.2 0.0 copy-start
  7.2 0.0 all-reduce.6.cloned.1.call-start
  7.2 1.5 bitcast_add_fusion
  8.7 0.0 copy-done
  8.7 0.7 convolution_bitcast_fusion
  9.4 33.8 %psum.44 = f32[64,128]{1,0:T(8,128)S(1)} all-reduce(f32[64,128]{1,0:T(8,128)S(1)} %convolution_bitcast_fusion), channel_id=1, replica_groups=mesh['replica'=4,'inner'=128] {'replica'}, use_global_device_ids=true, to_apply=%region_2.0 | all-reduce | flops 8192 | bytes 65536 | tf_op jit(solution)/shard_map/psum | solution.py:46
  43.2 0.2 fusion.8
  43.4 926.7 %psum.45 = f32[64,64]{0,1:T(8,128)S(1)} all-reduce(f32[64,64]{0,1:T(8,128)S(1)} %fusion.8), channel_id=1, replica_groups=mesh['replica'=4,'inner'=128] {'inner'}, use_global_device_ids=true, to_apply=%region_3.0 | all-reduce | flops 4096 | bytes 32768 | tf_op jit(solution)/shard_map/psum | solution.py:48
  970.1 0.1 copy.19
  970.2 5.8 cholesky.16
  976.1 0.6 compare_reduce_fusion
  976.7 0.7 fusion.3
  977.4 4.9 custom-call.6
  982.3 0.3 fusion.4
  982.5 0.0 copy-start.2
  982.5 0.0 copy-start.5
  982.6 1.1 fusion.17
  983.7 0.0 copy-done.2
  983.7 0.7 bitcast_subtract_fusion.1
  984.4 0.2 copy-done.4
  984.5 0.1 copy-done.8
  984.6 0.6 bitcast_subtract_fusion.2
  985.3 0.0 all-reduce.6.cloned.1.call-update
  985.3 0.0 all-reduce.4.cloned.1.call-start
  985.3 198.2 %all-reduce.6.cloned.1.call-done = (f32[2,8,1024]{2,1,0:T(8,128)}, f32[2,8,2048]{2,1,0:T(8,128)}, f32[64,1024]{1,0:T(8,128)}) async-done(((f32[2,8,1024]{2,1,0:T(8,128)}, f32[2,8,2048]{2,1,0:T(8,128)}, f32[64,1024]{1,0:T(8,128)}), (f32[2,8,1024]{2,1,0:T(8,128)}, f32[2,8,2048]{2,1,0:T(8,128)}, f32[64,1024]{1,0:T(8,128)})) %all-reduce.6.cloned.1.call-update) | async-done | bytes 458768 | tf_op jit(solution)/shard_map/psum | solution.py:44
  1183.6 0.0 all-reduce.4.cloned.1.call-update
  1183.6 0.0 copy-start.1
  1183.6 0.9 copy-done.7
  1184.5 0.7 multiply_subtract_fusion.1
  1185.2 1.5 multiply_subtract_fusion.2
  1186.7 1795.0 %all-reduce.4.cloned.1.call-done = f32[64,1024]{1,0:T(8,128)} async-done(((f32[64,1024]{1,0:T(8,128)}), f32[64,1024]{1,0:T(8,128)}) %all-reduce.4.cloned.1.call-update) | async-done | bytes 262160 | tf_op jit(solution)/shard_map/psum | solution.py:13
  2981.8 2.8 multiply_subtract_fusion
  (13 shorter events, 0.1 us)
Async XLA Ops:
  7.2 1.6 copy-start
  7.2 1176.4 %all-reduce.6.cloned.1.call-start = ((), (), s32[]{:S(2)}) async-start(), calls=%async_computation.1 | async-start | bytes 917504 | tf_op jit(solution)/shard_map/psum | solution.py:44
  982.5 1.2 copy-start.2
  982.5 1.2 copy-start.5
  983.7 0.8 copy-start.4
  983.7 0.9 copy-start.8
  985.3 198.4 %copy-start.6 = (f32[2,8,2048]{2,1,0:T(8,128)S(1)}, f32[2,8,2048]{2,1,0:T(8,128)}, u32[]{:S(2)}) copy-start(f32[2,8,2048]{2,1,0:T(8,128)} %param.16) | copy-start | bytes 393220
  985.3 1996.5 %all-reduce.4.cloned.1.call-start = ((), (), s32[]{:S(2)}) async-start(), calls=%async_computation | async-start | bytes 524288 | tf_op jit(solution)/shard_map/psum | solution.py:13
  1183.6 0.9 copy-start.7
  1183.6 1.6 copy-start.9
  1183.6 1798.2 %copy-start.3 = (f32[128,1024]{1,0:T(8,128)S(1)}, f32[128,1024]{1,0:T(8,128)}, u32[]{:S(2)}) copy-start(f32[128,1024]{1,0:T(8,128)} %param.19) | copy-start | bytes 1572868
  1183.6 1798.2 %copy-start.1 = (f32[128,1024]{1,0:T(8,128)S(1)}, f32[128,1024]{1,0:T(8,128)}, u32[]{:S(2)}) copy-start(f32[128,1024]{1,0:T(8,128)} %param.17) | copy-start | bytes 1572868
Sparse Core Ops, SparseCore 0:
  985.4 198.1 all-reduce.5
  1186.7 1794.9 all-reduce.3

commit v2 on v0

--- a/solution.py
+++ b/solution.py
@@ -33,7 +33,12 @@
     corrected = embed_weights - embed_copies[0] + embed_error[0]
     square_sum, broad_sum = lax.psum((square_term, broad_term), "replica")
     left_local = lax.dot_general(warm_start, corrected, contract_last, precision=highest)
-    left_factor = lax.psum(left_local, "replica") / replicas
+
+    def lift_local_data(block_here):
+        x_next = jnp.sum(jax.lax.all_gather(block_here, "replica"), 0)
+        return x_next
+
+    left_factor = lift_local_data(left_local) / replicas
     gram_local = lax.dot_general(left_factor, left_factor, contract_last, precision=highest)
     gram_matrix = lax.psum(gram_local, "inner")
     lower_factor = jnp.linalg.cholesky(gram_matrix)

time: 1640 us -> 1620 us (0.988)
    psum x1 -> x0, blocking collectives: 33.8 us -> none  [local(): left_factor = lax.psum(left_local, 'replica') / replicas]
    all_gather x0 -> x1, blocking collectives: none -> 20.8 us  [lift_local_data(): x_next = jnp.sum(jax.lax.all_gather(block_here, 'replica'), 0)]
where the time goes in v2:
time: 1620 us
  blocking collectives  947 us (58%)
  waiting for transfers between devices  637 us (39%)
  other arithmetic  17.2 us (1%)
    psum x1, blocking collectives, local(): gram_matrix = lax.psum(gram_local, 'inner')  926 us
    psum x1, waiting for transfers between devices, local(): right_total = lax.psum(right_term, ('replica', 'inner'))  557 us
    psum x1, waiting for transfers between devices, local(): square_sum, broad_sum = lax.psum((square_term, broad_term), 'replica')  79.8 us
  transfers between devices with their start and end apart: 2, of which 2 were waited for; matrix products, arithmetic and copies ran while one was open for 0% of the time, Pallas kernels for 0%

profile of v2, /device:TPU:1, one launch (start us, length us, event | category | flops | bytes accessed | tf_op | source)
XLA Modules:
  0.0 1621.0 jit_solution(15205912772731341858)
XLA Ops:
  7.2 0.0 copy-start
  7.2 0.0 all-reduce.4.cloned.1.call-start
  7.2 1.5 bitcast_add_fusion
  8.7 0.0 copy-done
  8.7 0.7 convolution_bitcast_fusion
  9.4 20.8 %all-gather = f32[256,128]{1,0:T(8,128)S(1)} all-gather(f32[64,128]{1,0:T(8,128)S(1)} %convolution_bitcast_fusion), channel_id=2, replica_groups=mesh['replica'=4,'inner'=128] {'replica'}, dimensions={0}, use_global_device_ids=true | all-gather | bytes 163840 | tf_op jit(solution)/shard_map/all_gather | solution.py:38
  30.3 0.2 fusion.8
  30.5 926.2 %psum.30 = f32[64,64]{0,1:T(8,128)S(1)} all-reduce(f32[64,64]{0,1:T(8,128)S(1)} %fusion.8), channel_id=1, replica_groups=mesh['replica'=4,'inner'=128] {'inner'}, use_global_device_ids=true, to_apply=%region_3.0 | all-reduce | flops 4096 | bytes 32768 | tf_op jit(solution)/shard_map/psum | solution.py:43
  956.7 0.1 copy.19
  956.8 5.8 cholesky.16
  962.6 0.6 compare_reduce_fusion
  963.3 0.7 fusion.3
  963.9 4.9 custom-call.6
  968.8 0.3 fusion.4
  969.1 0.0 copy-start.2
  969.1 0.0 copy-start.5
  969.1 0.0 copy-start.4
  969.1 0.0 copy-start.7
  969.1 1.1 fusion.17
  970.3 0.0 all-reduce.4.cloned.1.call-update
  970.3 0.0 all-reduce.6.cloned.1.call-start
  970.4 0.7 bitcast_subtract_fusion.1
  971.1 0.6 bitcast_subtract_fusion.2
  971.7 0.0 all-reduce.6.cloned.1.call-update
  971.7 0.0 copy-start.6
  971.7 557.5 %all-reduce.4.cloned.1.call-done = f32[64,1024]{1,0:T(8,128)} async-done(((f32[64,1024]{1,0:T(8,128)}), f32[64,1024]{1,0:T(8,128)}) %all-reduce.4.cloned.1.call-update) | async-done | bytes 262160 | tf_op jit(solution)/shard_map/psum | solution.py:47
  1529.2 2.8 multiply_subtract_fusion
  1532.0 79.8 %all-reduce.6.cloned.1.call-done = (f32[2,8,1024]{2,1,0:T(8,128)}, f32[2,8,2048]{2,1,0:T(8,128)}) async-done(((f32[2,8,1024]{2,1,0:T(8,128)}, f32[2,8,2048]{2,1,0:T(8,128)}), (f32[2,8,1024]{2,1,0:T(8,128)}, f32[2,8,2048]{2,1,0:T(8,128)})) %all-reduce.6.cloned.1.call-update) | async-done | bytes 196624 | tf_op jit(solution)/shard_map/psum | solution.py:34
  1611.8 0.0 copy-done.6
  1611.8 1.7 multiply_subtract_fusion.1
  1613.5 0.0 copy-done.9
  1613.5 0.7 multiply_subtract_fusion.2
  (14 shorter events, 0.1 us)
Async XLA Ops:
  7.2 1.6 copy-start
  7.2 1522.0 %all-reduce.4.cloned.1.call-start = ((), (), s32[]{:S(2)}) async-start(), calls=%async_computation | async-start | bytes 524288 | tf_op jit(solution)/shard_map/psum | solution.py:47
  969.1 1.3 copy-start.2
  969.1 1.3 copy-start.5
  969.1 1.9 copy-start.4
  969.1 1.9 copy-start.7
  970.3 558.9 %copy-start.1 = (f32[128,1024]{1,0:T(8,128)S(1)}, f32[128,1024]{1,0:T(8,128)}, u32[]{:S(2)}) copy-start(f32[128,1024]{1,0:T(8,128)} %param.17) | copy-start | bytes 1572868
  970.3 558.9 %copy-start.3 = (f32[128,1024]{1,0:T(8,128)S(1)}, f32[128,1024]{1,0:T(8,128)}, u32[]{:S(2)}) copy-start(f32[128,1024]{1,0:T(8,128)} %param.19) | copy-start | bytes 1572868
  970.3 641.5 %all-reduce.6.cloned.1.call-start = ((), (), s32[]{:S(2)}) async-start(), calls=%async_computation.1 | async-start | bytes 393216 | tf_op jit(solution)/shard_map/psum | solution.py:34
  971.7 640.1 %copy-start.6 = (f32[2,8,2048]{2,1,0:T(8,128)S(1)}, f32[2,8,2048]{2,1,0:T(8,128)}, u32[]{:S(2)}) copy-start(f32[2,8,2048]{2,1,0:T(8,128)} %param.16) | copy-start | bytes 393220
  1611.8 1.7 copy-start.8
  1611.8 1.7 copy-start.9
Sparse Core Ops, SparseCore 0:
  970.4 558.7 all-reduce.3
  1533.0 78.7 all-reduce.5
